TPU v7x, 32 devices: a whole 2x2x4 slice. The times are simulated.
32 devices in a mesh: groups: 2 (over y), space: 8 (over z, x), tm: 2 (over core).
Axes of the slice: x: 2, y: 2, z: 4, core: 2. Of those that a mesh axis runs over, the one named last changes fastest.
Arguments:
- base_latent: bfloat16 [64, 2, 12, 128], P(('groups', 'space'), 'tm'), parts along dimension 0, may hold values from -6 to 6
- cotangent: bfloat16 [64, 8, 48, 128], P(('groups', 'space'), 'tm'), parts along dimension 0, may hold values from -6 to 6
- w_spatial: bfloat16 [3, 3, 128, 128], replicated, may hold values from -0.1875 to 0.1875
- w_temporal: bfloat16 [5, 128, 128], replicated, may hold values from -0.25 to 0.25
Outputs:
- result: bfloat16 [64, 8, 48, 128], P(('groups', 'space'), 'tm'), parts along dimension 0
- grad_base: float32 [64, 2, 12, 128], P(('groups', 'space'), 'tm'), parts along dimension 0
- grad_spatial: float32 [6, 3, 128, 128], P('groups'), parts along dimension 0
- grad_temporal: float32 [10, 128, 128], P('groups'), parts along dimension 0
There are 2 independent parts, one for each index of `groups`. A program takes and returns all parts, laid end to end along the dimension named above; an argument that names none is the same for every part. Nothing has to cross between parts.
All inputs are finite; a program needn't handle non-finite values.
Results may differ from a plain program's by a relative error of at most 0.0064.
Values may be sent and summed in bfloat16 or wider, within the bound.
No kernel may reach another device: no remote copies, remote signals or barrier semaphores. Data moves between devices by JAX's collectives and lax.ppermute only.
A program may use at most 64 MiB of HBM per device.

v0:
```python
import jax
import jax.numpy as jnp
from jax import lax
from jax.sharding import PartitionSpec as P

FRAME_DILATION = 2


def shifted(value, axis, by):
    count = lax.axis_size(axis)
    pairs = [(i, i + by) for i in range(count) if 0 <= i + by < count]
    return lax.ppermute(value, axis, pairs)


def extended(cells, sides, width):
    for axis, dim in sides:
        count = lax.axis_size(axis)
        ends = count - 1
        head = lax.slice_in_dim(cells, 0, width, axis=dim)
        tail = lax.slice_in_dim(cells, cells.shape[dim] - width, cells.shape[dim], axis=dim)
        cells = jnp.concatenate(
            [
                lax.ppermute(tail, axis, [(i, (i + 1) % count) for i in range(ends)]),
                cells,
                lax.ppermute(head, axis, [((i + 1) % count, i) for i in range(ends)]),
            ],
            axis=dim,
        )
    return cells


def widen_cols(field):
    left_cols = jnp.concatenate([field[:, :, :1], field[:, :, :-1]], axis=2)
    right_cols = jnp.concatenate([field[:, :, 1:], field[:, :, -1:]], axis=2)
    phases = jnp.stack(
        [
            0.375 * left_cols + 0.625 * field,
            0.125 * left_cols + 0.875 * field,
            0.875 * field + 0.125 * right_cols,
            0.625 * field + 0.375 * right_cols,
        ],
        axis=3,
    )
    return phases.reshape(field.shape[0], field.shape[1], field.shape[2] * 4, field.shape[3])


def widen_rows(below_rows, middle, above_rows):
    phases = jnp.stack(
        [
            0.375 * below_rows + 0.625 * middle,
            0.125 * below_rows + 0.875 * middle,
            0.875 * middle + 0.125 * above_rows,
            0.625 * middle + 0.375 * above_rows,
        ],
        axis=2,
    )
    return phases.reshape(middle.shape[0], middle.shape[1] * 4, middle.shape[2], middle.shape[3])


def silu_slope(value):
    sigmoid_val = jax.nn.sigmoid(value)
    return sigmoid_val * (1.0 + value * (1.0 - sigmoid_val))


def conv_three(padded, weight, row_count, col_count, start):
    frame_count = padded.shape[0]
    channels = weight.shape[3]
    summed = jnp.zeros((frame_count * row_count * col_count, channels), jnp.float32)
    for tap_row in range(3):
        for tap_col in range(3):
            r0 = start - tap_row if start else tap_row
            c0 = start - tap_col if start else tap_col
            frame_window = padded[:, r0 : r0 + row_count, c0 : c0 + col_count].reshape(
                -1, padded.shape[3]
            )
            kernel = weight[tap_row, tap_col] if not start else weight[tap_row, tap_col].T
            summed = summed + jnp.dot(frame_window, kernel, preferred_element_type=jnp.float32)
    return summed.reshape(frame_count, row_count, col_count, channels)


def space_grads(padded, delta, row_count, col_count):
    flat = delta.reshape(-1, delta.shape[3])
    taps = []
    for tap_row in range(3):
        for tap_col in range(3):
            frame_window = padded[
                :, tap_row : tap_row + row_count, tap_col : tap_col + col_count
            ].reshape(-1, padded.shape[3])
            taps.append(
                lax.dot_general(
                    frame_window, flat, (((0,), (0,)), ((), ())), preferred_element_type=jnp.float32
                )
            )
    return jnp.stack(taps).reshape(3, 3, padded.shape[3], delta.shape[3])


def conv_time(frames_extended, weight, frame_count, reversed_order):
    channels = weight.shape[2]
    tensor_shape = frames_extended.shape
    summed = jnp.zeros((frame_count * tensor_shape[1] * tensor_shape[2], channels), jnp.float32)
    for kernel_tap in range(5):
        frame_offset = (
            (4 - kernel_tap) * FRAME_DILATION if reversed_order else kernel_tap * FRAME_DILATION
        )
        frame_window = frames_extended[frame_offset : frame_offset + frame_count].reshape(
            -1, tensor_shape[3]
        )
        kernel = weight[kernel_tap].T if reversed_order else weight[kernel_tap]
        summed = summed + jnp.dot(frame_window, kernel, preferred_element_type=jnp.float32)
    return summed.reshape(frame_count, tensor_shape[1], tensor_shape[2], channels)


def time_grads(frames_extended, delta, frame_count):
    flat = delta.reshape(-1, delta.shape[3])
    taps = []
    for kernel_tap in range(5):
        frame_window = frames_extended[
            kernel_tap * FRAME_DILATION : kernel_tap * FRAME_DILATION + frame_count
        ].reshape(-1, frames_extended.shape[3])
        taps.append(
            lax.dot_general(
                frame_window, flat, (((0,), (0,)), ((), ())), preferred_element_type=jnp.float32
            )
        )
    return jnp.stack(taps)


def shrink_base(grad_image, row_rank, row_devices, latent_shape):
    frame_count, low_rows, low_cols, channels = latent_shape
    _, col_pull = jax.vjp(
        widen_cols, jnp.zeros((frame_count, grad_image.shape[1], low_cols, channels), jnp.float32)
    )
    narrow = col_pull(grad_image)[0].reshape(frame_count, low_rows, 4, low_cols, channels)
    to_lower = 0.375 * narrow[:, :, 0] + 0.125 * narrow[:, :, 1]
    to_middle = (
        0.625 * narrow[:, :, 0]
        + 0.875 * narrow[:, :, 1]
        + 0.875 * narrow[:, :, 2]
        + 0.625 * narrow[:, :, 3]
    )
    to_upper = 0.125 * narrow[:, :, 2] + 0.375 * narrow[:, :, 3]
    from_above = shifted(to_lower, "tm", -1)
    from_below = shifted(to_upper, "tm", 1)
    next_lower = jnp.concatenate([to_lower[:, 1:], from_above], axis=1)
    prev_upper = jnp.concatenate([from_below, to_upper[:, :-1]], axis=1)
    edge_low = jnp.where(row_rank == 0, to_lower, jnp.zeros_like(to_lower))
    edge_high = jnp.where(row_rank == row_devices - 1, to_upper, jnp.zeros_like(to_upper))
    empty_rows = jnp.zeros((frame_count, low_rows - 1, low_cols, channels), jnp.float32)
    summed = to_middle + next_lower + prev_upper
    return (
        summed
        + jnp.concatenate([edge_low, empty_rows], axis=1)
        + jnp.concatenate([empty_rows, edge_high], axis=1)
    )


def local(base_latent, cotangent, w_spatial, w_temporal):
    row_rank = lax.axis_index("tm")
    row_devices = lax.axis_size("tm")
    padded_base = extended(base_latent, (("tm", 1),), 1)
    low_first = jnp.where(row_rank == 0, base_latent, padded_base[:, :1])
    high_last = jnp.where(row_rank == row_devices - 1, base_latent, padded_base[:, -1:])
    latent32 = base_latent.astype(jnp.float32)
    below_rows = jnp.concatenate([low_first, base_latent[:, :-1]], axis=1).astype(jnp.float32)
    above_rows = jnp.concatenate([base_latent[:, 1:], high_last], axis=1).astype(jnp.float32)
    upsampled = widen_cols(widen_rows(below_rows, latent32, above_rows)).astype(jnp.bfloat16)
    frame_count, row_count, col_count = (upsampled.shape[0], upsampled.shape[1], upsampled.shape[2])
    image_ext = extended(upsampled, (("tm", 1),), 1)
    padded = jnp.pad(image_ext, ((0, 0), (0, 0), (1, 1), (0, 0)))
    pre_one = conv_three(padded, w_spatial, row_count, col_count, 0)
    first_activation = jax.nn.silu(pre_one).astype(jnp.bfloat16)
    frames_extended = extended(first_activation, (("space", 0),), 2 * FRAME_DILATION)
    pre_two = conv_time(frames_extended, w_temporal, frame_count, False)
    result = (upsampled.astype(jnp.float32) + jax.nn.silu(pre_two)).astype(jnp.bfloat16)
    upstream = cotangent.astype(jnp.float32)
    second_gradient = (upstream * silu_slope(pre_two)).astype(jnp.bfloat16)
    temporal_local = time_grads(frames_extended, second_gradient, frame_count)
    grad_temporal = lax.psum(temporal_local, ("space", "tm"))
    gradient_extended = extended(second_gradient, (("space", 0),), 2 * FRAME_DILATION)
    back_one = conv_time(gradient_extended, w_temporal, frame_count, True)
    delta_one = (back_one * silu_slope(pre_one)).astype(jnp.bfloat16)
    spatial_local = space_grads(padded, delta_one, row_count, col_count)
    delta_rows = extended(delta_one, (("tm", 1),), 1)
    delta_pad = jnp.pad(delta_rows, ((0, 0), (0, 0), (1, 1), (0, 0)))
    grad_image = upstream + conv_three(delta_pad, w_spatial, row_count, col_count, 2)
    grad_base = shrink_base(grad_image, row_rank, row_devices, base_latent.shape)
    grad_spatial = lax.psum(spatial_local, ("space", "tm"))
    return (result, grad_base, grad_spatial, grad_temporal)


def solution(mesh):
    in_specs = (
        P(("groups", "space"), "tm", None, None),
        P(("groups", "space"), "tm", None, None),
        P(),
        P(),
    )
    out_specs = (
        P(("groups", "space"), "tm", None, None),
        P(("groups", "space"), "tm", None, None),
        P("groups", None, None, None),
        P("groups", None, None),
    )
    return jax.shard_map(local, mesh=mesh, in_specs=in_specs, out_specs=out_specs, check_vma=False)
```

profile of v0, /device:TPU:0, one launch (start us, length us, event | category | flops | bytes accessed | tf_op | source)
XLA Modules:
  0.0 162.9 jit_solution(3683068652345166377)
XLA Ops:
  7.2 0.8 copy.55
  8.0 2.4 %collective-permute-start = (bf16[4,1,12,128]{3,1,2,0:T(2,128)(2,1)S(1)}, bf16[4,1,12,128]{3,1,2,0:T(2,128)(2,1)S(1)}, u32[]{:S(2)}, u32[]{:S(2)}) collective-permute-start(bf16[4,1,12,128]{3,1,2,0:T(2,128)(2,1)S(1)} %copy.55), channel_id=1, source_target_pairs={{0,1},{2,3},{4,5},{6,7},{8,9},{10,11},{12,13},{14,15},{16,17},{18,... | collective-permute-start | bytes 36872 | tf_op jit(solution)/shard_map/ppermute | solution.py:23
  10.4 1.3 collective-permute-start.1
  11.7 1.8 %collective-permute-done.1 = bf16[4,1,12,128]{3,1,2,0:T(2,128)(2,1)S(1)} collective-permute-done((bf16[4,1,12,128]{3,1,2,0:T(2,128)(2,1)S(1)}, bf16[4,1,12,128]{3,1,2,0:T(2,128)(2,1)S(1)}, u32[]{:S(2)}, u32[]{:S(2)}) %collective-permute-start.1) | collective-permute-done | bytes 12320 | tf_op jit(solution)/shard_map/ppermute | solution.py:25
  14.4 2.1 %collective-permute-start.2 = (bf16[4,1,48,128]{3,2,1,0:T(8,128)(2,1)S(1)}, bf16[4,1,48,128]{3,2,1,0:T(8,128)(2,1)S(1)}, u32[]{:S(2)}, u32[]{:S(2)}) collective-permute-start(bf16[4,1,48,128]{3,2,1,0:T(8,128)(2,1)S(1)} %get-tuple-element.34), channel_id=1, source_target_pairs={{0,1},{2,3},{4,5},{6,7},{8,9},{10,11},{12,13},{14,15},{16,17},{18,... | collective-permute-start | bytes 147464 | tf_op jit(solution)/shard_map/ppermute | solution.py:23
  16.5 1.3 collective-permute-start.3
  17.8 1.8 %collective-permute-done.3 = bf16[4,1,48,128]{3,2,1,0:T(8,128)(2,1)S(1)} collective-permute-done((bf16[4,1,48,128]{3,2,1,0:T(8,128)(2,1)S(1)}, bf16[4,1,48,128]{3,2,1,0:T(8,128)(2,1)S(1)}, u32[]{:S(2)}, u32[]{:S(2)}) %collective-permute-start.3) | collective-permute-done | bytes 49184 | tf_op jit(solution)/shard_map/ppermute | solution.py:25
  19.9 0.8 copy-done
  22.7 4.2 %collective-permute-start.4 = (bf16[4,4,48,128]{3,2,1,0:T(8,128)(2,1)S(1)}, bf16[4,4,48,128]{3,2,1,0:T(8,128)(2,1)S(1)}, u32[]{:S(2)}, u32[]{:S(2)}) collective-permute-start(bf16[4,4,48,128]{3,2,1,0:T(8,128)(2,1)S(1)} %multiply_convert_fusion.3), channel_id=1, source_target_pairs={{0,2},{2,4},{4,6},{6,8},{8,10},{10,12},{12,14},{1,3},{3,5},{5,7},{... | collective-permute-start | bytes 589832 | tf_op jit(solution)/shard_map/ppermute | solution.py:23
  26.9 1.3 collective-permute-start.5
  28.4 3.0 %collective-permute-done.4 = bf16[4,4,48,128]{3,2,1,0:T(8,128)(2,1)S(1)} collective-permute-done((bf16[4,4,48,128]{3,2,1,0:T(8,128)(2,1)S(1)}, bf16[4,4,48,128]{3,2,1,0:T(8,128)(2,1)S(1)}, u32[]{:S(2)}, u32[]{:S(2)}) %collective-permute-start.4) | collective-permute-done | bytes 196640 | tf_op jit(solution)/shard_map/ppermute | solution.py:23
  31.4 4.0 %collective-permute-done.5 = bf16[4,4,48,128]{3,2,1,0:T(8,128)(2,1)S(1)} collective-permute-done((bf16[4,4,48,128]{3,2,1,0:T(8,128)(2,1)S(1)}, bf16[4,4,48,128]{3,2,1,0:T(8,128)(2,1)S(1)}, u32[]{:S(2)}, u32[]{:S(2)}) %collective-permute-start.5) | collective-permute-done | bytes 196640 | tf_op jit(solution)/shard_map/ppermute | solution.py:25
  36.3 0.7 copy-done.1
  37.0 0.9 fusion.21
  37.9 1.3 collective-permute-start.6
  39.2 5.1 %collective-permute-start.7 = (bf16[4,4,48,128]{3,2,1,0:T(8,128)(2,1)S(1)}, bf16[4,4,48,128]{3,2,1,0:T(8,128)(2,1)S(1)}, u32[]{:S(2)}, u32[]{:S(2)}) collective-permute-start(bf16[4,4,48,128]{3,2,1,0:T(8,128)(2,1)S(1)} %get-tuple-element.10), channel_id=1, source_target_pairs={{0,2},{2,4},{4,6},{6,8},{8,10},{10,12},{12,14},{1,3},{3,5},{5,7},{... | collective-permute-start | bytes 589832 | tf_op jit(solution)/shard_map/ppermute | solution.py:23
  45.9 0.6 collective-permute-done.6
  46.5 5.2 %collective-permute-done.7 = bf16[4,4,48,128]{3,2,1,0:T(8,128)(2,1)S(1)} collective-permute-done((bf16[4,4,48,128]{3,2,1,0:T(8,128)(2,1)S(1)}, bf16[4,4,48,128]{3,2,1,0:T(8,128)(2,1)S(1)}, u32[]{:S(2)}, u32[]{:S(2)}) %collective-permute-start.7) | collective-permute-done | bytes 196640 | tf_op jit(solution)/shard_map/ppermute | solution.py:23
  52.4 0.3 multiply_convert_fusion
  54.6 1.9 %collective-permute-start.8 = (bf16[4,1,48,128]{3,2,1,0:T(8,128)(2,1)S(1)}, bf16[4,1,48,128]{3,2,1,0:T(8,128)(2,1)S(1)}, u32[]{:S(2)}, u32[]{:S(2)}) collective-permute-start(bf16[4,1,48,128]{3,2,1,0:T(8,128)(2,1)S(1)} %get-tuple-element.26), channel_id=1, source_target_pairs={{0,1},{2,3},{4,5},{6,7},{8,9},{10,11},{12,13},{14,15},{16,17},{18,... | collective-permute-start | bytes 147464 | tf_op jit(solution)/shard_map/ppermute | solution.py:23
  56.6 1.3 collective-permute-start.9
  58.4 0.8 copy-done.2
  59.2 0.5 collective-permute-done.9
  62.0 0.3 fusion.122
  62.5 0.6 copy-done.7
  63.3 1.3 collective-permute-start.10
  64.6 3.0 %collective-permute-start.11 = (f32[4,1,12,128]{3,1,2,0:T(1,128)S(1)}, f32[4,1,12,128]{3,1,2,0:T(1,128)S(1)}, u32[]{:S(2)}, u32[]{:S(2)}) collective-permute-start(f32[4,1,12,128]{3,1,2,0:T(1,128)S(1)} %get-tuple-element.40), channel_id=1, source_target_pairs={{0,1},{2,3},{4,5},{6,7},{8,9},{10,11},{12,13},{14,15},{16,17},{18,... | collective-permute-start | bytes 73736 | tf_op jit(solution)/shard_map/ppermute | solution.py:12
  67.7 0.8 collective-permute-done.11
  68.5 0.7 fusion.107
  69.2 84.1 %all-reduce.8.cloned.1.call-done = (f32[3,3,128,128]{3,2,1,0:T(8,128)}, f32[5,128,128]{2,1,0:T(8,128)}) async-done(((f32[3,3,128,128]{3,2,1,0:T(8,128)}, f32[5,128,128]{2,1,0:T(8,128)}), (f32[3,3,128,128]{3,2,1,0:T(8,128)}, f32[5,128,128]{2,1,0:T(8,128)})) %all-reduce.8.cloned.1.call-update) | async-done | bytes 917520 | tf_op jit(solution)/shard_map/psum | solution.py:187
  153.4 2.0 %copy.127 = f32[3,3,128,128]{3,2,1,0:T(8,128)} copy(f32[3,3,128,128]{3,2,1,0:T(8,128)} %get-tuple-element.58) | data formatting | bytes 1179648
  155.3 0.7 copy.128
  (86 shorter events, 11.3 us)
Async XLA Ops:
  7.2 146.2 %all-reduce.8.cloned.1.call-start = ((), (), s32[]{:S(2)}) async-start(), calls=%async_computation | async-start | bytes 1835008 | tf_op jit(solution)/shard_map/psum | solution.py:187
  7.2 6.3 %copy-start.6 = (bf16[4,1,12,128]{3,0,2,1:T(4,128)(2,1)S(1)}, bf16[4,1,12,128]{3,0,2,1:T(4,128)(2,1)}, u32[]{:S(2)}) copy-start(bf16[4,1,12,128]{3,0,2,1:T(4,128)(2,1)} %param.4) | copy-start | bytes 36868
  8.0 3.7 %collective-permute-start = (bf16[4,1,12,128]{3,1,2,0:T(2,128)(2,1)S(1)}, bf16[4,1,12,128]{3,1,2,0:T(2,128)(2,1)S(1)}, u32[]{:S(2)}, u32[]{:S(2)}) collective-permute-start(bf16[4,1,12,128]{3,1,2,0:T(2,128)(2,1)S(1)} %copy.55), channel_id=1, source_target_pairs={{0,1},{2,3},{4,5},{6,7},{8,9},{10,11},{12,13},{14,15},{16,17},{18,... | collective-permute-start | bytes 36872 | tf_op jit(solution)/shard_map/ppermute | solution.py:23
  10.4 3.1 %collective-permute-start.1 = (bf16[4,1,12,128]{3,1,2,0:T(2,128)(2,1)S(1)}, bf16[4,1,12,128]{3,1,2,0:T(2,128)(2,1)S(1)}, u32[]{:S(2)}, u32[]{:S(2)}) collective-permute-start(bf16[4,1,12,128]{3,1,2,0:T(2,128)(2,1)S(1)} %copy.55), channel_id=1, source_target_pairs={{1,0},{3,2},{5,4},{7,6},{9,8},{11,10},{13,12},{15,14},{17,16},{19,... | collective-permute-start | bytes 36872 | tf_op jit(solution)/shard_map/ppermute | solution.py:25
  14.4 3.4 %collective-permute-start.2 = (bf16[4,1,48,128]{3,2,1,0:T(8,128)(2,1)S(1)}, bf16[4,1,48,128]{3,2,1,0:T(8,128)(2,1)S(1)}, u32[]{:S(2)}, u32[]{:S(2)}) collective-permute-start(bf16[4,1,48,128]{3,2,1,0:T(8,128)(2,1)S(1)} %get-tuple-element.34), channel_id=1, source_target_pairs={{0,1},{2,3},{4,5},{6,7},{8,9},{10,11},{12,13},{14,15},{16,17},{18,... | collective-permute-start | bytes 147464 | tf_op jit(solution)/shard_map/ppermute | solution.py:23
  16.5 3.1 %collective-permute-start.3 = (bf16[4,1,48,128]{3,2,1,0:T(8,128)(2,1)S(1)}, bf16[4,1,48,128]{3,2,1,0:T(8,128)(2,1)S(1)}, u32[]{:S(2)}, u32[]{:S(2)}) collective-permute-start(bf16[4,1,48,128]{3,2,1,0:T(8,128)(2,1)S(1)} %get-tuple-element.35), channel_id=1, source_target_pairs={{1,0},{3,2},{5,4},{7,6},{9,8},{11,10},{13,12},{15,14},{17,16},{19,... | collective-permute-start | bytes 147464 | tf_op jit(solution)/shard_map/ppermute | solution.py:25
  19.7 1.0 copy-start
  22.5 5.7 %copy-start.3 = (bf16[5,128,128]{2,1,0:T(8,128)(2,1)S(1)}, bf16[5,128,128]{2,1,0:T(8,128)(2,1)}, u32[]{:S(2)}) copy-start(bf16[5,128,128]{2,1,0:T(8,128)(2,1)} %param.7) | copy-start | bytes 491524
  22.7 8.8 %collective-permute-start.4 = (bf16[4,4,48,128]{3,2,1,0:T(8,128)(2,1)S(1)}, bf16[4,4,48,128]{3,2,1,0:T(8,128)(2,1)S(1)}, u32[]{:S(2)}, u32[]{:S(2)}) collective-permute-start(bf16[4,4,48,128]{3,2,1,0:T(8,128)(2,1)S(1)} %multiply_convert_fusion.3), channel_id=1, source_target_pairs={{0,2},{2,4},{4,6},{6,8},{8,10},{10,12},{12,14},{1,3},{3,5},{5,7},{... | collective-permute-start | bytes 589832 | tf_op jit(solution)/shard_map/ppermute | solution.py:23
  26.9 8.6 %collective-permute-start.5 = (bf16[4,4,48,128]{3,2,1,0:T(8,128)(2,1)S(1)}, bf16[4,4,48,128]{3,2,1,0:T(8,128)(2,1)S(1)}, u32[]{:S(2)}, u32[]{:S(2)}) collective-permute-start(bf16[4,4,48,128]{3,2,1,0:T(8,128)(2,1)S(1)} %multiply_convert_fusion.3), channel_id=1, source_target_pairs={{2,0},{4,2},{6,4},{8,6},{10,8},{12,10},{14,12},{3,1},{5,3},{7,5},{... | collective-permute-start | bytes 589832 | tf_op jit(solution)/shard_map/ppermute | solution.py:25
  36.1 0.9 copy-start.1
  37.9 8.5 %collective-permute-start.6 = (bf16[4,4,48,128]{3,2,1,0:T(8,128)(2,1)S(1)}, bf16[4,4,48,128]{3,2,1,0:T(8,128)(2,1)S(1)}, u32[]{:S(2)}, u32[]{:S(2)}) collective-permute-start(bf16[4,4,48,128]{3,2,1,0:T(8,128)(2,1)S(1)} %get-tuple-element.10), channel_id=1, source_target_pairs={{2,0},{4,2},{6,4},{8,6},{10,8},{12,10},{14,12},{3,1},{5,3},{7,5},{... | collective-permute-start | bytes 589832 | tf_op jit(solution)/shard_map/ppermute | solution.py:25
  39.2 12.4 %collective-permute-start.7 = (bf16[4,4,48,128]{3,2,1,0:T(8,128)(2,1)S(1)}, bf16[4,4,48,128]{3,2,1,0:T(8,128)(2,1)S(1)}, u32[]{:S(2)}, u32[]{:S(2)}) collective-permute-start(bf16[4,4,48,128]{3,2,1,0:T(8,128)(2,1)S(1)} %get-tuple-element.10), channel_id=1, source_target_pairs={{0,2},{2,4},{4,6},{6,8},{8,10},{10,12},{12,14},{1,3},{3,5},{5,7},{... | collective-permute-start | bytes 589832 | tf_op jit(solution)/shard_map/ppermute | solution.py:23
  45.9 5.8 %copy-start.4 = (f32[5,128,128]{2,1,0:T(8,128)}, f32[5,128,128]{2,1,0:T(8,128)S(1)}, u32[]{:S(2)}) copy-start(f32[5,128,128]{2,1,0:T(8,128)S(1)} %fusion.10) | copy-start | bytes 983044
  54.6 4.6 %collective-permute-start.8 = (bf16[4,1,48,128]{3,2,1,0:T(8,128)(2,1)S(1)}, bf16[4,1,48,128]{3,2,1,0:T(8,128)(2,1)S(1)}, u32[]{:S(2)}, u32[]{:S(2)}) collective-permute-start(bf16[4,1,48,128]{3,2,1,0:T(8,128)(2,1)S(1)} %get-tuple-element.26), channel_id=1, source_target_pairs={{0,1},{2,3},{4,5},{6,7},{8,9},{10,11},{12,13},{14,15},{16,17},{18,... | collective-permute-start | bytes 147464 | tf_op jit(solution)/shard_map/ppermute | solution.py:23
  56.6 3.1 %collective-permute-start.9 = (bf16[4,1,48,128]{3,2,1,0:T(8,128)(2,1)S(1)}, bf16[4,1,48,128]{3,2,1,0:T(8,128)(2,1)S(1)}, u32[]{:S(2)}, u32[]{:S(2)}) collective-permute-start(bf16[4,1,48,128]{3,2,1,0:T(8,128)(2,1)S(1)} %get-tuple-element.27), channel_id=1, source_target_pairs={{1,0},{3,2},{5,4},{7,6},{9,8},{11,10},{13,12},{15,14},{17,16},{19,... | collective-permute-start | bytes 147464 | tf_op jit(solution)/shard_map/ppermute | solution.py:25
  58.4 0.8 copy-start.2
  62.4 0.7 copy-start.7
  63.3 4.3 %collective-permute-start.10 = (f32[4,1,12,128]{3,1,2,0:T(1,128)S(1)}, f32[4,1,12,128]{3,1,2,0:T(1,128)S(1)}, u32[]{:S(2)}, u32[]{:S(2)}) collective-permute-start(f32[4,1,12,128]{3,1,2,0:T(1,128)S(1)} %get-tuple-element.41), channel_id=1, source_target_pairs={{1,0},{3,2},{5,4},{7,6},{9,8},{11,10},{13,12},{15,14},{17,16},{19,... | collective-permute-start | bytes 73736 | tf_op jit(solution)/shard_map/ppermute | solution.py:12
  64.6 3.9 %collective-permute-start.11 = (f32[4,1,12,128]{3,1,2,0:T(1,128)S(1)}, f32[4,1,12,128]{3,1,2,0:T(1,128)S(1)}, u32[]{:S(2)}, u32[]{:S(2)}) collective-permute-start(f32[4,1,12,128]{3,1,2,0:T(1,128)S(1)} %get-tuple-element.40), channel_id=1, source_target_pairs={{0,1},{2,3},{4,5},{6,7},{8,9},{10,11},{12,13},{14,15},{16,17},{18,... | collective-permute-start | bytes 73736 | tf_op jit(solution)/shard_map/ppermute | solution.py:12
  153.4 2.0 %copy-start.5 = (f32[5,128,128]{2,1,0:T(8,128)S(1)}, f32[5,128,128]{2,1,0:T(8,128)}, u32[]{:S(2)}) copy-start(f32[5,128,128]{2,1,0:T(8,128)} %get-tuple-element.59) | copy-start | bytes 983044
Sparse Core Ops, SparseCore 0:
  59.3 93.9 all-reduce.7
where the time goes:
time: 163 us
  waiting for transfers between devices  102 us (63%)
  starting transfers between devices  26.5 us (16%)
  between operations  14.7 us (9%)
  matrix products  9.25 us (6%)
  local copies, waits for them, and re-layouts  7.29 us (4%)
  other arithmetic  3.34 us (2%)
    psum x1, waiting for transfers between devices, local(): grad_spatial = lax.psum(spatial_local, ('space', 'tm'))  84.1 us
    ppermute x5, starting transfers between devices, extended(): lax.ppermute(tail, axis, [(i, (i + 1) % count) for i in range(ends)])  15.7 us
    ppermute x5, waiting for transfers between devices, extended(): lax.ppermute(head, axis, [((i + 1) % count, i) for i in range(ends)])  8.69 us
    ppermute x5, waiting for transfers between devices, extended(): lax.ppermute(tail, axis, [(i, (i + 1) % count) for i in range(ends)])  8.19 us
    ppermute x5, starting transfers between devices, extended(): lax.ppermute(head, axis, [((i + 1) % count, i) for i in range(ends)])  6.45 us
    unnamed x19, local copies, waits for them, and re-layouts  6.45 us
    ppermute x2, starting transfers between devices, shifted(): return lax.ppermute(value, axis, pairs)  4.32 us
    dot_general x18, matrix products, conv_three(): jnp.dot(frame_window, kernel, preferred_element_type=jnp.float32)  3.61 us
  transfers between devices with their start and end apart: 13, of which 9 were waited for; matrix products, arithmetic and copies ran while one was open for 4% of the time, Pallas kernels for 0%

commit v1 on v0

--- a/solution.py
+++ b/solution.py
@@ -184,7 +184,9 @@
     delta_pad = jnp.pad(delta_rows, ((0, 0), (0, 0), (1, 1), (0, 0)))
     grad_image = upstream + conv_three(delta_pad, w_spatial, row_count, col_count, 2)
     grad_base = shrink_base(grad_image, row_rank, row_devices, base_latent.shape)
-    grad_spatial = lax.psum(spatial_local, ("space", "tm"))
+    grad_spatial = spatial_local
+    for mesh_axis in ("tm", "space"):
+        grad_spatial = lax.psum(grad_spatial, mesh_axis)
     return (result, grad_base, grad_spatial, grad_temporal)
 
 

time: 163 us -> 257 us (1.58)
  waiting for transfers between devices: 102 us -> 195 us
    psum x1 -> x3, waiting for transfers between devices: 84.1 us -> 177 us  [the longest x2 89.7 us: local(): grad_spatial = lax.psum(grad_spatial, mesh_axis)]
  transfers between devices with their start and end apart: 13 -> 15, of which waited for: 9 -> 11; matrix products, arithmetic and copies ran while one was open for 4% -> 2% of each run, Pallas kernels for 0% -> 0%
where the time goes in v1:
time: 257 us
  waiting for transfers between devices  195 us (76%)
  starting transfers between devices  26.6 us (10%)
  between operations  14.4 us (6%)
  matrix products  9.25 us (4%)
  local copies, waits for them, and re-layouts  8 us (3%)
  other arithmetic  3.36 us (1%)
    psum x2, waiting for transfers between devices, local(): grad_spatial = lax.psum(grad_spatial, mesh_axis)  89.7 us
    psum x1, waiting for transfers between devices, local(): grad_temporal = lax.psum(temporal_local, ('space', 'tm'))  87.1 us
    ppermute x5, starting transfers between devices, extended(): lax.ppermute(tail, axis, [(i, (i + 1) % count) for i in range(ends)])  15.7 us
    ppermute x5, waiting for transfers between devices, extended(): lax.ppermute(head, axis, [((i + 1) % count, i) for i in range(ends)])  9.51 us
    ppermute x5, waiting for transfers between devices, extended(): lax.ppermute(tail, axis, [(i, (i + 1) % count) for i in range(ends)])  8.18 us
    unnamed x19, local copies, waits for them, and re-layouts  7.16 us
    ppermute x5, starting transfers between devices, extended(): lax.ppermute(head, axis, [((i + 1) % count, i) for i in range(ends)])  6.45 us
  transfers between devices with their start and end apart: 15, of which 11 were waited for; matrix products, arithmetic and copies ran while one was open for 2% of the time, Pallas kernels for 0%

profile of v1, /device:TPU:0, one launch (start us, length us, event | category | flops | bytes accessed | tf_op | source)
XLA Modules:
  0.0 257.0 jit_solution(4809223432138061681)
XLA Ops:
  7.2 0.8 copy.55
  8.0 2.4 collective-permute-start
  10.4 1.3 collective-permute-start.1
  11.7 1.8 collective-permute-done.1
  14.4 2.1 collective-permute-start.2
  16.5 1.3 collective-permute-start.3
  17.8 1.8 collective-permute-done.3
  19.9 0.8 copy-done
  22.7 4.2 %collective-permute-start.4 = (bf16[4,4,48,128]{3,2,1,0:T(8,128)(2,1)S(1)}, bf16[4,4,48,128]{3,2,1,0:T(8,128)(2,1)S(1)}, u32[]{:S(2)}, u32[]{:S(2)}) collective-permute-start(bf16[4,4,48,128]{3,2,1,0:T(8,128)(2,1)S(1)} %multiply_convert_fusion.3), channel_id=1, source_target_pairs={{0,2},{2,4},{4,6},{6,8},{8,10},{10,12},{12,14},{1,3},{3,5},{5,7},{... | collective-permute-start | bytes 589832 | tf_op jit(solution)/shard_map/ppermute | solution.py:23
  26.9 1.3 collective-permute-start.5
  28.4 3.0 %collective-permute-done.4 = bf16[4,4,48,128]{3,2,1,0:T(8,128)(2,1)S(1)} collective-permute-done((bf16[4,4,48,128]{3,2,1,0:T(8,128)(2,1)S(1)}, bf16[4,4,48,128]{3,2,1,0:T(8,128)(2,1)S(1)}, u32[]{:S(2)}, u32[]{:S(2)}) %collective-permute-start.4) | collective-permute-done | bytes 196640 | tf_op jit(solution)/shard_map/ppermute | solution.py:23
  31.4 4.0 %collective-permute-done.5 = bf16[4,4,48,128]{3,2,1,0:T(8,128)(2,1)S(1)} collective-permute-done((bf16[4,4,48,128]{3,2,1,0:T(8,128)(2,1)S(1)}, bf16[4,4,48,128]{3,2,1,0:T(8,128)(2,1)S(1)}, u32[]{:S(2)}, u32[]{:S(2)}) %collective-permute-start.5) | collective-permute-done | bytes 196640 | tf_op jit(solution)/shard_map/ppermute | solution.py:25
  36.3 0.7 copy-done.1
  37.1 0.9 fusion.21
  38.0 1.3 collective-permute-start.6
  39.2 5.1 %collective-permute-start.7 = (bf16[4,4,48,128]{3,2,1,0:T(8,128)(2,1)S(1)}, bf16[4,4,48,128]{3,2,1,0:T(8,128)(2,1)S(1)}, u32[]{:S(2)}, u32[]{:S(2)}) collective-permute-start(bf16[4,4,48,128]{3,2,1,0:T(8,128)(2,1)S(1)} %get-tuple-element.8), channel_id=1, source_target_pairs={{0,2},{2,4},{4,6},{6,8},{8,10},{10,12},{12,14},{1,3},{3,5},{5,7},{... | collective-permute-start | bytes 589832 | tf_op jit(solution)/shard_map/ppermute | solution.py:23
  45.4 1.1 collective-permute-done.6
  46.5 5.2 %collective-permute-done.7 = bf16[4,4,48,128]{3,2,1,0:T(8,128)(2,1)S(1)} collective-permute-done((bf16[4,4,48,128]{3,2,1,0:T(8,128)(2,1)S(1)}, bf16[4,4,48,128]{3,2,1,0:T(8,128)(2,1)S(1)}, u32[]{:S(2)}, u32[]{:S(2)}) %collective-permute-start.7) | collective-permute-done | bytes 196640 | tf_op jit(solution)/shard_map/ppermute | solution.py:23
  55.1 0.8 copy-done.2
  56.3 1.9 collective-permute-start.8
  58.2 1.3 collective-permute-start.9
  59.8 0.7 copy-done.5
  60.6 0.8 collective-permute-done.9
  64.1 12.4 %all-reduce.9.cloned.1.call-done = f32[3,3,128,128]{3,2,1,0:T(8,128)} async-done(((f32[3,3,128,128]{3,2,1,0:T(8,128)}), f32[3,3,128,128]{3,2,1,0:T(8,128)}) %all-reduce.9.cloned.1.call-update) | async-done | bytes 589840 | tf_op jit(solution)/shard_map/psum | solution.py:189
  77.4 1.3 collective-permute-start.10
  78.7 3.0 %collective-permute-start.11 = (f32[4,1,12,128]{3,1,2,0:T(1,128)S(1)}, f32[4,1,12,128]{3,1,2,0:T(1,128)S(1)}, u32[]{:S(2)}, u32[]{:S(2)}) collective-permute-start(f32[4,1,12,128]{3,1,2,0:T(1,128)S(1)} %get-tuple-element.38), channel_id=1, source_target_pairs={{0,1},{2,3},{4,5},{6,7},{8,9},{10,11},{12,13},{14,15},{16,17},{18,... | collective-permute-start | bytes 73736 | tf_op jit(solution)/shard_map/ppermute | solution.py:12
  81.7 0.8 collective-permute-done.11
  82.5 0.7 fusion.107
  83.3 87.1 %all-reduce.13.cloned.1.call-done = f32[5,128,128]{2,1,0:T(8,128)} async-done(((f32[5,128,128]{2,1,0:T(8,128)}), f32[5,128,128]{2,1,0:T(8,128)}) %all-reduce.13.cloned.1.call-update) | async-done | bytes 327696 | tf_op jit(solution)/shard_map/psum | solution.py:178
  170.4 77.3 %all-reduce.11.cloned.1.call-done = f32[3,3,128,128]{3,2,1,0:T(8,128)} async-done(((f32[3,3,128,128]{3,2,1,0:T(8,128)}), f32[3,3,128,128]{3,2,1,0:T(8,128)}) %all-reduce.11.cloned.1.call-update) | async-done | bytes 589840 | tf_op jit(solution)/shard_map/psum | solution.py:189
  247.7 2.0 copy.128
  249.7 0.7 copy.129
  (92 shorter events, 12.7 us)
Async XLA Ops:
  7.2 69.3 %all-reduce.9.cloned.1.call-start = ((), (), s32[]{:S(2)}) async-start(), calls=%async_computation | async-start | bytes 1179648 | tf_op jit(solution)/shard_map/psum | solution.py:189
  7.2 6.3 %copy-start.6 = (bf16[4,1,12,128]{3,0,2,1:T(4,128)(2,1)S(1)}, bf16[4,1,12,128]{3,0,2,1:T(4,128)(2,1)}, u32[]{:S(2)}) copy-start(bf16[4,1,12,128]{3,0,2,1:T(4,128)(2,1)} %param.4) | copy-start | bytes 36868
  8.0 3.7 %collective-permute-start = (bf16[4,1,12,128]{3,1,2,0:T(2,128)(2,1)S(1)}, bf16[4,1,12,128]{3,1,2,0:T(2,128)(2,1)S(1)}, u32[]{:S(2)}, u32[]{:S(2)}) collective-permute-start(bf16[4,1,12,128]{3,1,2,0:T(2,128)(2,1)S(1)} %copy.55), channel_id=1, source_target_pairs={{0,1},{2,3},{4,5},{6,7},{8,9},{10,11},{12,13},{14,15},{16,17},{18,... | collective-permute-start | bytes 36872 | tf_op jit(solution)/shard_map/ppermute | solution.py:23
  10.4 3.1 %collective-permute-start.1 = (bf16[4,1,12,128]{3,1,2,0:T(2,128)(2,1)S(1)}, bf16[4,1,12,128]{3,1,2,0:T(2,128)(2,1)S(1)}, u32[]{:S(2)}, u32[]{:S(2)}) collective-permute-start(bf16[4,1,12,128]{3,1,2,0:T(2,128)(2,1)S(1)} %copy.55), channel_id=1, source_target_pairs={{1,0},{3,2},{5,4},{7,6},{9,8},{11,10},{13,12},{15,14},{17,16},{19,... | collective-permute-start | bytes 36872 | tf_op jit(solution)/shard_map/ppermute | solution.py:25
  14.4 3.4 %collective-permute-start.2 = (bf16[4,1,48,128]{3,2,1,0:T(8,128)(2,1)S(1)}, bf16[4,1,48,128]{3,2,1,0:T(8,128)(2,1)S(1)}, u32[]{:S(2)}, u32[]{:S(2)}) collective-permute-start(bf16[4,1,48,128]{3,2,1,0:T(8,128)(2,1)S(1)} %get-tuple-element.32), channel_id=1, source_target_pairs={{0,1},{2,3},{4,5},{6,7},{8,9},{10,11},{12,13},{14,15},{16,17},{18,... | collective-permute-start | bytes 147464 | tf_op jit(solution)/shard_map/ppermute | solution.py:23
  16.5 3.1 %collective-permute-start.3 = (bf16[4,1,48,128]{3,2,1,0:T(8,128)(2,1)S(1)}, bf16[4,1,48,128]{3,2,1,0:T(8,128)(2,1)S(1)}, u32[]{:S(2)}, u32[]{:S(2)}) collective-permute-start(bf16[4,1,48,128]{3,2,1,0:T(8,128)(2,1)S(1)} %get-tuple-element.33), channel_id=1, source_target_pairs={{1,0},{3,2},{5,4},{7,6},{9,8},{11,10},{13,12},{15,14},{17,16},{19,... | collective-permute-start | bytes 147464 | tf_op jit(solution)/shard_map/ppermute | solution.py:25
  19.7 1.0 copy-start
  22.5 5.7 %copy-start.3 = (bf16[5,128,128]{2,1,0:T(8,128)(2,1)S(1)}, bf16[5,128,128]{2,1,0:T(8,128)(2,1)}, u32[]{:S(2)}) copy-start(bf16[5,128,128]{2,1,0:T(8,128)(2,1)} %param.7) | copy-start | bytes 491524
  22.7 8.8 %collective-permute-start.4 = (bf16[4,4,48,128]{3,2,1,0:T(8,128)(2,1)S(1)}, bf16[4,4,48,128]{3,2,1,0:T(8,128)(2,1)S(1)}, u32[]{:S(2)}, u32[]{:S(2)}) collective-permute-start(bf16[4,4,48,128]{3,2,1,0:T(8,128)(2,1)S(1)} %multiply_convert_fusion.3), channel_id=1, source_target_pairs={{0,2},{2,4},{4,6},{6,8},{8,10},{10,12},{12,14},{1,3},{3,5},{5,7},{... | collective-permute-start | bytes 589832 | tf_op jit(solution)/shard_map/ppermute | solution.py:23
  26.9 8.6 %collective-permute-start.5 = (bf16[4,4,48,128]{3,2,1,0:T(8,128)(2,1)S(1)}, bf16[4,4,48,128]{3,2,1,0:T(8,128)(2,1)S(1)}, u32[]{:S(2)}, u32[]{:S(2)}) collective-permute-start(bf16[4,4,48,128]{3,2,1,0:T(8,128)(2,1)S(1)} %multiply_convert_fusion.3), channel_id=1, source_target_pairs={{2,0},{4,2},{6,4},{8,6},{10,8},{12,10},{14,12},{3,1},{5,3},{7,5},{... | collective-permute-start | bytes 589832 | tf_op jit(solution)/shard_map/ppermute | solution.py:25
  36.1 0.9 copy-start.1
  38.0 8.5 %collective-permute-start.6 = (bf16[4,4,48,128]{3,2,1,0:T(8,128)(2,1)S(1)}, bf16[4,4,48,128]{3,2,1,0:T(8,128)(2,1)S(1)}, u32[]{:S(2)}, u32[]{:S(2)}) collective-permute-start(bf16[4,4,48,128]{3,2,1,0:T(8,128)(2,1)S(1)} %get-tuple-element.8), channel_id=1, source_target_pairs={{2,0},{4,2},{6,4},{8,6},{10,8},{12,10},{14,12},{3,1},{5,3},{7,5},{... | collective-permute-start | bytes 589832 | tf_op jit(solution)/shard_map/ppermute | solution.py:25
  39.2 12.4 %collective-permute-start.7 = (bf16[4,4,48,128]{3,2,1,0:T(8,128)(2,1)S(1)}, bf16[4,4,48,128]{3,2,1,0:T(8,128)(2,1)S(1)}, u32[]{:S(2)}, u32[]{:S(2)}) collective-permute-start(bf16[4,4,48,128]{3,2,1,0:T(8,128)(2,1)S(1)} %get-tuple-element.8), channel_id=1, source_target_pairs={{0,2},{2,4},{4,6},{6,8},{8,10},{10,12},{12,14},{1,3},{3,5},{5,7},{... | collective-permute-start | bytes 589832 | tf_op jit(solution)/shard_map/ppermute | solution.py:23
  55.1 0.8 copy-start.2
  56.0 114.4 %all-reduce.13.cloned.1.call-start = ((), (), s32[]{:S(2)}) async-start(), calls=%async_computation.2 | async-start | bytes 655360 | tf_op jit(solution)/shard_map/psum | solution.py:178
  56.3 4.3 %collective-permute-start.8 = (bf16[4,1,48,128]{3,2,1,0:T(8,128)(2,1)S(1)}, bf16[4,1,48,128]{3,2,1,0:T(8,128)(2,1)S(1)}, u32[]{:S(2)}, u32[]{:S(2)}) collective-permute-start(bf16[4,1,48,128]{3,2,1,0:T(8,128)(2,1)S(1)} %get-tuple-element.24), channel_id=1, source_target_pairs={{0,1},{2,3},{4,5},{6,7},{8,9},{10,11},{12,13},{14,15},{16,17},{18,... | collective-permute-start | bytes 147464 | tf_op jit(solution)/shard_map/ppermute | solution.py:23
  58.2 3.1 %collective-permute-start.9 = (bf16[4,1,48,128]{3,2,1,0:T(8,128)(2,1)S(1)}, bf16[4,1,48,128]{3,2,1,0:T(8,128)(2,1)S(1)}, u32[]{:S(2)}, u32[]{:S(2)}) collective-permute-start(bf16[4,1,48,128]{3,2,1,0:T(8,128)(2,1)S(1)} %get-tuple-element.25), channel_id=1, source_target_pairs={{1,0},{3,2},{5,4},{7,6},{9,8},{11,10},{13,12},{15,14},{17,16},{19,... | collective-permute-start | bytes 147464 | tf_op jit(solution)/shard_map/ppermute | solution.py:25
  59.8 0.7 copy-start.5
  60.5 187.2 %all-reduce.11.cloned.1.call-start = ((), (), s32[]{:S(2)}) async-start(), calls=%async_computation.1 | async-start | bytes 1179648 | tf_op jit(solution)/shard_map/psum | solution.py:189
  76.5 0.7 copy-start.7
  77.4 4.3 %collective-permute-start.10 = (f32[4,1,12,128]{3,1,2,0:T(1,128)S(1)}, f32[4,1,12,128]{3,1,2,0:T(1,128)S(1)}, u32[]{:S(2)}, u32[]{:S(2)}) collective-permute-start(f32[4,1,12,128]{3,1,2,0:T(1,128)S(1)} %get-tuple-element.39), channel_id=1, source_target_pairs={{1,0},{3,2},{5,4},{7,6},{9,8},{11,10},{13,12},{15,14},{17,16},{19,... | collective-permute-start | bytes 73736 | tf_op jit(solution)/shard_map/ppermute | solution.py:12
  78.7 3.9 %collective-permute-start.11 = (f32[4,1,12,128]{3,1,2,0:T(1,128)S(1)}, f32[4,1,12,128]{3,1,2,0:T(1,128)S(1)}, u32[]{:S(2)}, u32[]{:S(2)}) collective-permute-start(f32[4,1,12,128]{3,1,2,0:T(1,128)S(1)} %get-tuple-element.38), channel_id=1, source_target_pairs={{0,1},{2,3},{4,5},{6,7},{8,9},{10,11},{12,13},{14,15},{16,17},{18,... | collective-permute-start | bytes 73736 | tf_op jit(solution)/shard_map/ppermute | solution.py:12
  247.7 2.0 copy-start.4
Sparse Core Ops, SparseCore 0:
  56.1 20.3 all-reduce.8
  80.8 89.5 all-reduce.12
  173.8 73.9 all-reduce.10
